TPU v7x, 256 devices: a whole 4x4x8 slice. The times are simulated.
256 devices in a mesh: row: 32 (over z, y_hi, core), col: 8 (over x, y_lo).
Axes of the slice: x: 4, y: 4 (y_hi: 2, y_lo: 2; y = y_hi * 2 + y_lo), z: 8, core: 2. Of those that a mesh axis runs over, the one named last changes fastest.
Arguments:
- velocity: float32 [3, 32, 1024, 1024], P(None, None, 'row', 'col'), may hold values from -6 to 6
- dy_op: bfloat16 [1024, 1024], replicated, may hold values from -0.1875 to 0.1875
- dz_op: bfloat16 [1024, 1024], replicated, may hold values from -0.1875 to 0.1875
- node_force: float32 [3, 2048], P(None, ('row', 'col')), may hold values from -6 to 6
- node_cell: int32 [3, 2048], P(None, ('row', 'col')), may hold values from 0 to 1023, as said below
Outputs:
- tendency: float32 [3, 32, 1024, 1024], P(None, None, 'row', 'col')
Inputs may be any that keep to these rules, and one draw needn't show every extreme that they name: `node_cell`: the nodes of the block held by device (r, c) of the mesh have their z coordinate in the c-th of the 8 equal ranges of z; x lies below 32, y below 1024.
All inputs are finite; a program needn't handle non-finite values.
Results may differ from a plain program's by a relative error of at most 0.0029.
Values sent between devices are 32-bit elements; how exact they have to be, the bound alone decides.
A program may use at most 384 MiB of HBM per device.

v0:
```python
import jax
import jax.numpy as jnp
from jax import lax
from jax.sharding import PartitionSpec as P


def y_terms(pencil_slab, dy_op):
    transport_array = pencil_slab[1]
    result_list = []
    for comp in range(3):
        rounded = pencil_slab[comp].astype(jnp.bfloat16)
        gradient_in_y = jnp.einsum(
            "ab,xbz->xaz", dy_op, rounded, preferred_element_type=jnp.float32
        )
        result_list.append(-(transport_array * gradient_in_y))
    return jnp.stack(result_list)


def z_terms(pencil_slab, dz_op):
    transport_array = pencil_slab[2]
    result_list = []
    for comp in range(3):
        rounded = pencil_slab[comp].astype(jnp.bfloat16)
        gradient_in_z = jnp.einsum(
            "xyb,ab->xya", rounded, dz_op, preferred_element_type=jnp.float32
        )
        result_list.append(-(transport_array * gradient_in_z))
    return jnp.stack(result_list)


def per_device(velocity, dy_op, dz_op, node_force, node_cell):
    lines_y = lax.all_to_all(velocity, "row", split_axis=1, concat_axis=2, tiled=True)
    along_y = y_terms(lines_y, dy_op)
    summed = along_y + lax.all_to_all(
        z_terms(lax.all_to_all(lines_y, "col", split_axis=2, concat_axis=3, tiled=True), dz_op),
        "col",
        split_axis=3,
        concat_axis=2,
        tiled=True,
    )
    tendency = lax.all_to_all(summed, "row", split_axis=2, concat_axis=1, tiled=True)
    forces, node_cells = (
        lax.all_gather(node_force, "row", axis=1, tiled=True),
        lax.all_gather(node_cell, "row", axis=1, tiled=True),
    )
    y_direction_width = tendency.shape[2]
    width_z = tendency.shape[3]
    row_pos = lax.axis_index("row")
    col_pos = lax.axis_index("col")
    local_y = node_cells[1] - row_pos * y_direction_width
    local_z = node_cells[2] - col_pos * width_z
    owned_node = (
        (local_y >= 0) & (local_y < y_direction_width) & (local_z >= 0) & (local_z < width_z)
    )
    flat_index = jnp.where(
        owned_node, (node_cells[0] * y_direction_width + local_y) * width_z + local_z, 0
    ).astype(jnp.int32)
    pushed = jnp.where(owned_node[None], forces, jnp.float32(0.0))
    flat_out = tendency.reshape(3, -1).at[:, flat_index].add(pushed)
    return flat_out.reshape(tendency.shape)


def solution(mesh):
    return jax.shard_map(
        per_device,
        mesh=mesh,
        in_specs=(
            P(None, None, "row", "col"),
            P(),
            P(),
            P(None, ("row", "col")),
            P(None, ("row", "col")),
        ),
        out_specs=P(None, None, "row", "col"),
        check_vma=False,
    )
```

profile of v0, /device:TPU:1, one launch (start us, length us, event | category | flops | bytes accessed | tf_op | source)
XLA Modules:
  0.0 368.4 jit_solution(18316489696962972272)
XLA Ops:
  0.0 1.7 copy.72
  1.7 52.3 %all_to_all.54 = f32[3,32,32,128]{3,2,0,1:T(8,128)S(1)} all-to-all(f32[3,32,32,128]{3,2,0,1:T(8,128)S(1)} %copy.72), channel_id=1, replica_groups=mesh['row'=32,'col'=8] {'row'}, dimensions={1} | all-to-all | bytes 3145728 | tf_op jit(solution)/shard_map/all_to_all | solution.py:32
  54.1 1.0 copy-done.2
  55.1 1.6 copy.78
  56.8 23.3 %all_to_all.55 = f32[3,1,1024,128]{3,1,0,2:T(1,128)S(1)} all-to-all(f32[3,1,1024,128]{3,1,0,2:T(1,128)S(1)} %copy.78), channel_id=1, replica_groups=mesh['row'=32,'col'=8] {'col'}, dimensions={2} | all-to-all | bytes 3145728 | tf_op jit(solution)/shard_map/all_to_all | solution.py:35
  80.4 0.9 copy.81
  81.6 0.9 fusion.11
  82.5 1.7 fusion.15
  84.2 0.9 copy.82
  85.0 1.9 fusion.13
  86.9 1.3 pad_maximum_fusion
  88.2 4.9 %copy.83 = f32[3,1,128,1024]{2,1,0,3:T(1,128)} copy(f32[3,1,128,1024]{3,2,1,0:T(8,128)} %pad_maximum_fusion) | data formatting | bytes 3145728 | tf_op jit(solution)/shard_map/stack | solution.py:28
  93.1 4.3 %all-to-all-start.2 = ((f32[3,1,128,1024]{2,1,0,3:T(1,128)}), f32[3,1,128,1024]{2,1,0,3:T(1,128)}, u32[]{:S(2)}, u32[]{:S(2)}) async-start(f32[3,1,128,1024]{2,1,0,3:T(1,128)} %copy.83), calls=%async_computation.2 | async-start | bytes 3145728 | tf_op jit(solution)/shard_map/all_to_all | solution.py:34
  97.4 1.1 slice.78
  98.5 1.1 slice.51
  99.8 1.7 convert.8
  101.8 0.8 fusion.9
  102.7 1.7 fusion.7
  104.3 1.7 fusion.5
  106.0 12.4 %all-to-all-done.2 = f32[3,1,128,1024]{2,1,0,3:T(1,128)} async-done(((f32[3,1,128,1024]{2,1,0,3:T(1,128)}), f32[3,1,128,1024]{2,1,0,3:T(1,128)}, u32[]{:S(2)}, u32[]{:S(2)}) %all-to-all-start.2) | async-done | bytes 1572896 | tf_op jit(solution)/shard_map/all_to_all | solution.py:34
  118.4 1.5 copy.84
  119.9 2.1 copy.85
  122.0 2.6 all_to_all.48
  124.6 2.9 maximum_add_fusion
  127.5 4.9 %copy.86 = f32[3,1,1024,128]{3,1,0,2:T(1,128)} copy(f32[3,1,1024,128]{2,3,1,0:T(8,128)} %maximum_add_fusion) | data formatting | bytes 3145728 | tf_op jit(solution)/shard_map/add | solution.py:34
  132.4 10.1 %all-to-all-start.3 = ((f32[3,1,1024,128]{3,1,0,2:T(1,128)}), f32[3,1,1024,128]{3,1,0,2:T(1,128)}, u32[]{:S(2)}, u32[]{:S(2)}) async-start(f32[3,1,1024,128]{3,1,0,2:T(1,128)} %copy.86), calls=%async_computation.3 | async-start | bytes 3145728 | tf_op jit(solution)/shard_map/all_to_all | solution.py:41
  142.6 68.3 %all-gather.1 = f32[32,8,3]{1,2,0:T(4,128)S(1)} all-gather(f32[1,8,3]{1,2,0:T(4,128)S(1)} %bitcast.110), channel_id=1, replica_groups=mesh['row'=32,'col'=8] {'row'}, dimensions={0}, use_global_device_ids=true | all-gather | bytes 3168 | tf_op jit(solution)/shard_map/all_gather | solution.py:43
  210.9 38.8 %all-gather = s32[32,8,3]{1,2,0:T(4,128)S(1)} all-gather(s32[1,8,3]{1,2,0:T(4,128)S(1)} %bitcast.111), channel_id=1, replica_groups=mesh['row'=32,'col'=8] {'row'}, dimensions={0}, use_global_device_ids=true | all-gather | bytes 3168 | tf_op jit(solution)/shard_map/all_gather | solution.py:44
  250.1 2.5 sort
  252.7 31.1 %copy.93 = f32[3,1,1024,128]{0,3,2,1:T(8,128)} copy(f32[3,1,1024,128]{3,1,0,2:T(1,128)} %all-to-all-done.3) | data formatting | bytes 3145728 | tf_op jit(solution)/shard_map/reshape | solution.py:59
  283.8 47.0 %scatter_custom_fusion = f32[3,131072]{0,1:T(8,128)} fusion(f32[3,131072]{0,1:T(8,128)} %bitcast.24, s32[256]{0:T(256)S(1)} %get-tuple-element.5, f32[256,3]{1,0:T(8,128)S(1)} %copy.91, s32[1024]{0:T(1024)S(1)} %pad_clamp_fusion), kind=kCustom, calls=%fused_computation.27 | custom fusion | flops 768 | bytes 1572864 | tf_op jit(solution)/shard_map/scatter-add | solution.py:59
  330.8 37.6 %copy.92 = f32[3,32,32,128]{3,2,1,0:T(8,128)} copy(f32[3,32,32,128]{0,3,2,1:T(8,128)} %bitcast.32) | data formatting | bytes 3145728 | tf_op jit(solution)/shard_map/reshape | solution.py:60
  (36 shorter events, 1.9 us)
Async XLA Ops:
  0.0 81.5 %copy-start = (bf16[1024,1024]{1,0:T(8,128)(2,1)S(1)}, bf16[1024,1024]{1,0:T(8,128)(2,1)}, u32[]{:S(2)}) copy-start(bf16[1024,1024]{1,0:T(8,128)(2,1)} %param.7) | copy-start | bytes 6291460
  53.9 1.2 copy-start.2
  55.1 1.6 copy-start.3
  81.6 1.0 copy-start.6
  85.0 1.9 copy-start.5
  93.1 25.3 %all-to-all-start.2 = ((f32[3,1,128,1024]{2,1,0,3:T(1,128)}), f32[3,1,128,1024]{2,1,0,3:T(1,128)}, u32[]{:S(2)}, u32[]{:S(2)}) async-start(f32[3,1,128,1024]{2,1,0,3:T(1,128)} %copy.83), calls=%async_computation.2 | async-start | bytes 3145728 | tf_op jit(solution)/shard_map/all_to_all | solution.py:34
  99.8 2.1 copy-start.1
  122.0 2.6 copy-start.4
  132.4 10.1 %copy-start.7 = (f32[3,8]{1,0:T(4,128)S(1)}, f32[3,8]{1,0:T(4,128)}, u32[]{:S(2)}) copy-start(f32[3,8]{1,0:T(4,128)} %param.8) | copy-start | bytes 292
  132.4 78.5 %copy-start.8 = (s32[3,8]{1,0:T(4,128)S(1)}, s32[3,8]{1,0:T(4,128)}, u32[]{:S(2)}) copy-start(s32[3,8]{1,0:T(4,128)} %param.9) | copy-start | bytes 292
  132.4 120.3 %all-to-all-start.3 = ((f32[3,1,1024,128]{3,1,0,2:T(1,128)}), f32[3,1,1024,128]{3,1,0,2:T(1,128)}, u32[]{:S(2)}, u32[]{:S(2)}) async-start(f32[3,1,1024,128]{3,1,0,2:T(1,128)} %copy.86), calls=%async_computation.3 | async-start | bytes 3145728 | tf_op jit(solution)/shard_map/all_to_all | solution.py:41
where the time goes:
time: 370 us; the launch traced here: 368 us
  blocking collectives  183 us (49%)
  local copies, waits for them, and re-layouts  94.4 us (26%)
  other arithmetic  55.8 us (15%)
  starting transfers between devices  14.4 us (4%)
  waiting for transfers between devices  12.4 us (3%)
  matrix products  8.52 us (2%)
    all_gather x1, blocking collectives, per_device(): lax.all_gather(node_force, 'row', axis=1, tiled=True)  68.3 us
    all_to_all x1, blocking collectives, per_device(): lax.all_to_all(velocity, 'row', split_axis=1, concat_axis=2, tiled=True)  52.3 us
    scatter-add x3, other arithmetic, per_device(): flat_out = tendency.reshape(3, -1).at[:, flat_index].add(pushed)  49.6 us
    all_gather x1, blocking collectives, per_device(): lax.all_gather(node_cell, 'row', axis=1, tiled=True)  38.8 us
    reshape x1, local copies, waits for them, and re-layouts, per_device(): return flat_out.reshape(tendency.shape)  37.6 us
    reshape x1, local copies, waits for them, and re-layouts, per_device(): flat_out = tendency.reshape(3, -1).at[:, flat_index].add(pushed)  31.1 us
    all_to_all x1, blocking collectives, per_device(): lax.all_to_all(lines_y, 'col', split_axis=2, concat_axis=3, tiled=True)  23.3 us
    all_to_all x1, waiting for transfers between devices, per_device(): lax.all_to_all(z_terms(lax.all_to_all(lines_y, 'col', split_axis=2, conca...  12.4 us
  transfers between devices with their start and end apart: 2, of which 1 were waited for; matrix products, arithmetic and copies ran while one was open for 3% of the time, Pallas kernels for 0%

commit v1 on v0

v1 whole, which is shorter than its diff:
```python
import functools

import jax
import jax.numpy as jnp
from jax import lax
from jax.experimental import pallas as pl
from jax.experimental.pallas import tpu as pltpu
from jax.sharding import PartitionSpec as P

MESH = pl.DeviceIdType.MESH
F32 = jnp.float32
BF16 = jnp.bfloat16
COMPS = 3


def kernel(
    n_row, n_col,
    vel, dy_hbm, dz_hbm, force, cell,
    out,
    dy, dz, vw, y_in, z_in, y_out, z_out, y_back, z_back, node_tile, node_all, delta,
    load_sem, y_in_sem, z_in_sem, y_back_sem, z_back_sem, node_sem,
    y_in_send, z_in_send, y_back_send, z_back_send, node_send,
):
    r = lax.axis_index("row")
    c = lax.axis_index("col")
    ny, nz = vel.shape[2], vel.shape[3]
    planes = vel.shape[1] // n_col
    n_nodes = force.shape[1]

    barrier = pltpu.get_barrier_semaphore()

    @pl.loop(1, n_row)
    def _(s):
        pl.semaphore_signal(
            barrier, inc=1, device_id={"row": lax.rem(r + s, n_row)}, device_id_type=MESH
        )

    @pl.loop(1, n_col)
    def _(s):
        pl.semaphore_signal(
            barrier, inc=1, device_id={"col": lax.rem(c + s, n_col)}, device_id_type=MESH
        )

    load_dy = pltpu.make_async_copy(dy_hbm, dy, load_sem.at[0])
    load_dz = pltpu.make_async_copy(dz_hbm, dz, load_sem.at[1])
    load_vw = pltpu.make_async_copy(vel.at[pl.ds(1, 2)], vw, load_sem.at[2])

    group = (n_row * n_nodes) // 128
    per_tile = n_row // group
    lane = lax.broadcasted_iota(jnp.int32, (COMPS, 128), 1)
    base = lax.rem(r, per_tile) * n_nodes
    forces, cells = force[...], cell[...].astype(F32)
    spread_f = jnp.zeros((COMPS, 128), F32)
    spread_c = jnp.zeros((COMPS, 128), F32)
    for k in range(n_nodes):
        spread_f = jnp.where(lane == base + k, forces[:, k : k + 1], spread_f)
        spread_c = jnp.where(lane == base + k, cells[:, k : k + 1], spread_c)
    node_tile[...] = jnp.zeros_like(node_tile)
    node_tile[0:COMPS, :] = spread_f
    node_tile[4 : 4 + COMPS, :] = spread_c

    pl.semaphore_wait(barrier, n_row + n_col - 2)

    for k in range(COMPS):

        @pl.loop(1, n_row)
        def _(s):
            to = lax.rem(r + s, n_row)
            pltpu.make_async_remote_copy(
                src_ref=vel.at[k, to],
                dst_ref=y_in.at[k, pl.ds(pl.multiple_of(r * ny, ny), ny)],
                send_sem=y_in_send.at[k],
                recv_sem=y_in_sem.at[k],
                device_id={"row": to},
                device_id_type=MESH,
            ).start()

        @pl.loop(1, n_col)
        def _(s):
            to = lax.rem(c + s, n_col)
            pltpu.make_async_remote_copy(
                src_ref=vel.at[k, pl.ds(to * planes, planes)],
                dst_ref=z_in.at[k, c],
                send_sem=z_in_send.at[k],
                recv_sem=z_in_sem.at[k],
                device_id={"col": to},
                device_id_type=MESH,
            ).start()

        pltpu.make_async_copy(
            vel.at[k, r], y_in.at[k, pl.ds(pl.multiple_of(r * ny, ny), ny)], y_in_sem.at[k]
        ).start()
        pltpu.make_async_copy(
            vel.at[k, pl.ds(c * planes, planes)], z_in.at[k, c], z_in_sem.at[k]
        ).start()
        if k == 0:
            load_dy.start()
            load_dz.start()
            load_vw.start()

            @pl.loop(1, n_row)
            def _(s):
                pltpu.make_async_remote_copy(
                    src_ref=node_tile,
                    dst_ref=node_all.at[r],
                    send_sem=node_send,
                    recv_sem=node_sem,
                    device_id={"row": lax.rem(r + s, n_row)},
                    device_id_type=MESH,
                ).start()

            pltpu.make_async_copy(node_tile, node_all.at[r], node_sem).start()

    load_dy.wait()
    load_dz.wait()
    for k in range(COMPS):
        pltpu.make_async_copy(y_in.at[k], y_in.at[k], y_in_sem.at[k]).wait()
        lines = y_in[k].astype(BF16)
        rows = 256 if dy.shape[0] % 256 == 0 else dy.shape[0]
        for m in range(dy.shape[0] // rows):
            y_out[k, m * rows : (m + 1) * rows, :] = jnp.dot(
                dy[m * rows : (m + 1) * rows, :], lines, preferred_element_type=F32
            )

        @pl.loop(1, n_row)
        def _(s):
            to = lax.rem(r + s, n_row)
            pltpu.make_async_remote_copy(
                src_ref=y_out.at[k, pl.ds(pl.multiple_of(to * ny, ny), ny)],
                dst_ref=y_back.at[k, r],
                send_sem=y_back_send.at[k],
                recv_sem=y_back_sem.at[k],
                device_id={"row": to},
                device_id_type=MESH,
            ).start()

        pltpu.make_async_copy(
            y_out.at[k, pl.ds(pl.multiple_of(r * ny, ny), ny)], y_back.at[k, r], y_back_sem.at[k]
        ).start()

        pltpu.make_async_copy(z_in.at[k], z_in.at[k], z_in_sem.at[k]).wait()
        lines = jnp.concatenate(
            [z_in[k, j].reshape(planes * ny, nz) for j in range(n_col)], axis=1
        ).astype(BF16)
        for j in range(n_col):
            z_out[k, j] = lax.dot_general(
                lines, dz[j * nz : (j + 1) * nz, :], (((1,), (1,)), ((), ())),
                preferred_element_type=F32,
            ).reshape(planes, ny, nz)

        @pl.loop(1, n_col)
        def _(s):
            to = lax.rem(c + s, n_col)
            pltpu.make_async_remote_copy(
                src_ref=z_out.at[k, to],
                dst_ref=z_back.at[k, pl.ds(c * planes, planes)],
                send_sem=z_back_send.at[k],
                recv_sem=z_back_sem.at[k],
                device_id={"col": to},
                device_id_type=MESH,
            ).start()

        pltpu.make_async_copy(
            z_out.at[k, c], z_back.at[k, pl.ds(c * planes, planes)], z_back_sem.at[k]
        ).start()

    pltpu.make_async_copy(node_all, node_all, node_sem).wait()
    tiles = []
    for g in range(group):
        total = node_all[g * per_tile]
        for j in range(1, per_tile):
            total = total + node_all[g * per_tile + j]
        tiles.append(total)
    nodes = jnp.concatenate(tiles, axis=1)
    count = 128 * group
    first_y = (r * ny).astype(F32)
    first_z = (c * nz).astype(F32)
    local_y = nodes[5:6, :] - first_y
    owned = (local_y >= 0.0) & (local_y < float(ny))
    key = jnp.where(owned, nodes[4:5, :] * float(ny) + local_y, -1.0)
    key_z = nodes[6:7, :] - first_z
    z_pos = lax.broadcasted_iota(jnp.int32, (nz, count), 0).astype(F32)
    hot_z = jnp.where(z_pos == key_z, 1.0, 0.0).astype(BF16)
    high = nodes.astype(BF16).astype(F32)
    rest = nodes - high
    mid = rest.astype(BF16).astype(F32)
    low = rest - mid
    rows = vel.shape[1] * ny
    step = 256 if rows % 256 == 0 else rows

    @pl.loop(0, rows // step)
    def _(m):
        pos = (lax.broadcasted_iota(jnp.int32, (step, count), 0) + m * step).astype(F32)
        hit = pos == key
        for k in range(COMPS):
            total = jnp.zeros((step, nz), F32)
            for part in (high, mid, low):
                pushed = jnp.where(hit, part[k : k + 1, :], 0.0).astype(BF16)
                total = total + lax.dot_general(
                    pushed, hot_z, (((1,), (1,)), ((), ())), preferred_element_type=F32
                )
            delta[k, pl.ds(pl.multiple_of(m * step, step), step), :] = total

    load_vw.wait()
    for k in range(COMPS):
        pltpu.make_async_copy(y_back.at[k], y_back.at[k], y_back_sem.at[k]).wait()
        pltpu.make_async_copy(z_back.at[k], z_back.at[k], z_back_sem.at[k]).wait()
        out[k] = delta[k].reshape(out.shape[1:]) - (vw[0] * y_back[k] + vw[1] * z_back[k])

    for k in range(COMPS):
        y_sent = y_in.at[k, pl.ds(0, (n_row - 1) * ny)]
        z_sent = z_in.at[k, pl.ds(0, n_col - 1)]
        pltpu.make_async_copy(y_sent, y_sent, y_in_send.at[k]).wait()
        pltpu.make_async_copy(z_sent, z_sent, z_in_send.at[k]).wait()
        pltpu.make_async_copy(y_sent, y_sent, y_back_send.at[k]).wait()
        pltpu.make_async_copy(z_sent, z_sent, z_back_send.at[k]).wait()
    nodes_sent = node_all.at[pl.ds(0, n_row - 1)]
    pltpu.make_async_copy(nodes_sent, nodes_sent, node_send).wait()


def per_device(n_row, n_col, velocity, dy_op, dz_op, node_force, node_cell):
    _, n_x, ny, nz = velocity.shape
    planes = n_x // n_col
    dma = pltpu.SemaphoreType.DMA
    hbm = pl.BlockSpec(memory_space=pl.ANY)
    vmem = pl.BlockSpec(memory_space=pltpu.VMEM)
    return pl.pallas_call(
        functools.partial(kernel, n_row, n_col),
        out_shape=jax.ShapeDtypeStruct(velocity.shape, F32),
        in_specs=[hbm, hbm, hbm, vmem, vmem],
        out_specs=vmem,
        scratch_shapes=[
            pltpu.VMEM(dy_op.shape, BF16),
            pltpu.VMEM(dz_op.shape, BF16),
            pltpu.VMEM((2, n_x, ny, nz), F32),
            pltpu.VMEM((COMPS, n_row * ny, nz), F32),
            pltpu.VMEM((COMPS, n_col, planes, ny, nz), F32),
            pltpu.VMEM((COMPS, n_row * ny, nz), F32),
            pltpu.VMEM((COMPS, n_col, planes, ny, nz), F32),
            pltpu.VMEM((COMPS, n_x, ny, nz), F32),
            pltpu.VMEM((COMPS, n_x, ny, nz), F32),
            pltpu.VMEM((8, 128), F32),
            pltpu.VMEM((n_row, 8, 128), F32),
            pltpu.VMEM((COMPS, n_x * ny, nz), F32),
            dma((3,)), dma((COMPS,)), dma((COMPS,)), dma((COMPS,)), dma((COMPS,)), dma(()),
            dma((COMPS,)), dma((COMPS,)), dma((COMPS,)), dma((COMPS,)), dma(()),
        ],
        compiler_params=pltpu.CompilerParams(
            collective_id=0, has_side_effects=True, vmem_limit_bytes=48 * 1024 * 1024
        ),
    )(velocity, dy_op, dz_op, node_force, node_cell)


def solution(mesh):
    return jax.shard_map(
        functools.partial(per_device, mesh.shape["row"], mesh.shape["col"]),
        mesh=mesh,
        in_specs=(
            P(None, None, "row", "col"),
            P(),
            P(),
            P(None, ("row", "col")),
            P(None, ("row", "col")),
        ),
        out_specs=P(None, None, "row", "col"),
        check_vma=False,
    )
```

time: 370 us -> 90.6 us (0.24)
  blocking collectives: 183 us -> 0 us
  local copies, waits for them, and re-layouts: 94.4 us -> 5.51 us
  Pallas kernels: 0 us -> 84.9 us
  other arithmetic: 55.8 us -> 0 us
  starting transfers between devices: 14.4 us -> 0 us
  waiting for transfers between devices: 12.4 us -> 0 us
  matrix products: 8.52 us -> 0 us
    all_gather x2 -> x0, blocking collectives: 107 us -> none  [the longest x1 68.3 us: per_device(): lax.all_gather(node_force, 'row', axis=1, tiled=True)]
    pallas_call x0 -> x1, Pallas kernels: none -> 84.9 us  [per_device(): pl.pallas_call(functools.partial(kernel, n_row, n_col), out_shape=jax.Sha...]
    all_to_all x2 -> x0, blocking collectives: 75.6 us -> none  [the longest x1 52.3 us: per_device(): lax.all_to_all(velocity, 'row', split_axis=1, concat_axis=2, tiled=True)]
    reshape x2 -> x0, local copies, waits for them, and re-layouts: 68.6 us -> none  [the longest x1 37.6 us: per_device(): return flat_out.reshape(tendency.shape)]
    scatter-add x3 -> x0, other arithmetic: 49.6 us -> none  [per_device(): flat_out = tendency.reshape(3, -1).at[:, flat_index].add(pushed)]
    all_to_all x2 -> x0, starting transfers between devices: 14.4 us -> none  [the longest x1 10.1 us: per_device(): lax.all_to_all(summed, 'row', split_axis=2, concat_axis=1, tiled=True)]
    all_to_all x2 -> x0, waiting for transfers between devices: 12.4 us -> none  [the longest x1 12.4 us: per_device(): lax.all_to_all(z_terms(lax.all_to_all(lines_y, 'col', split_axis=2, conca...]
    dot_general x6 -> x0, matrix products: 8.52 us -> none  [the longest x3 4.36 us: z_terms(): jnp.einsum('xyb,ab->xya', rounded, dz_op, preferred_element_type=jnp.floa...]
  transfers between devices with their start and end apart: 2 -> 0, of which waited for: 1 -> 0; matrix products, arithmetic and copies ran while one was open for 3% -> 0% of each run, Pallas kernels for 0% -> 0%
where the time goes in v1:
time: 90.6 us; the launch traced here: 90.5 us
  Pallas kernels  84.9 us (94%)
  local copies, waits for them, and re-layouts  5.51 us (6%)
    pallas_call x1, Pallas kernels, per_device(): pl.pallas_call(functools.partial(kernel, n_row, n_col), out_shape=jax.Sha...  84.9 us
    unnamed x9, local copies, waits for them, and re-layouts  5.51 us

profile of v1, /device:TPU:1, one launch (start us, length us, event | category | flops | bytes accessed | tf_op | source)
XLA Modules:
  0.0 90.5 jit_solution(1629489983905023924)
XLA Ops:
  0.0 0.0 copy-start
  0.0 1.6 %copy-done = bf16[1024,1024]{1,0:T(8,128)(2,1)S(1)} copy-done((bf16[1024,1024]{1,0:T(8,128)(2,1)S(1)}, bf16[1024,1024]{1,0:T(8,128)(2,1)}, u32[]{:S(2)}) %copy-start) | copy-done | bytes 2097176
  1.6 0.0 copy-start.1
  1.6 1.4 %copy-done.1 = f32[3,32,32,128]{3,2,1,0:T(8,128)S(1)} copy-done((f32[3,32,32,128]{3,2,1,0:T(8,128)S(1)}, f32[3,32,32,128]{3,2,1,0:T(8,128)}, u32[]{:S(2)}) %copy-start.1) | copy-done | bytes 1572888
  3.0 0.0 copy-start.2
  3.0 0.7 copy-done.2
  3.7 0.0 copy-start.3
  3.7 0.7 copy-done.3
  4.4 84.9 %shard_map.55 = f32[3,32,32,128]{3,2,1,0:T(8,128)S(1)} custom-call(f32[3,32,32,128]{3,2,1,0:T(8,128)S(1)} %copy-done.1, bf16[1024,1024]{1,0:T(8,128)(2,1)S(1)} %copy-done, bf16[1024,1024]{1,0:T(8,128)(2,1)} %dz_hbm.1, f32[3,8]{1,0:T(4,128)S(1)} %copy-done.2, s32[3,8]{1,0:T(4,128)S(1)} %copy-done.3), custom_call_target="tpu_custom_call" | custom-call | tf_op jit(solution)/shard_map/pallas_call | solution.py:227
  89.3 1.1 %copy.7 = f32[3,32,32,128]{3,2,1,0:T(8,128)} copy(f32[3,32,32,128]{3,2,1,0:T(8,128)S(1)} %shard_map.55) | data formatting | bytes 3145728
Async XLA Ops:
  0.0 1.6 %copy-start = (bf16[1024,1024]{1,0:T(8,128)(2,1)S(1)}, bf16[1024,1024]{1,0:T(8,128)(2,1)}, u32[]{:S(2)}) copy-start(bf16[1024,1024]{1,0:T(8,128)(2,1)} %dy_hbm.1) | copy-start | bytes 6291460
  1.6 1.4 %copy-start.1 = (f32[3,32,32,128]{3,2,1,0:T(8,128)S(1)}, f32[3,32,32,128]{3,2,1,0:T(8,128)}, u32[]{:S(2)}) copy-start(f32[3,32,32,128]{3,2,1,0:T(8,128)} %vel.1) | copy-start | bytes 4718596
  3.0 0.7 copy-start.2
  3.7 0.7 copy-start.3

commit v2 on v1

--- a/solution.py
+++ b/solution.py
@@ -15,9 +15,9 @@
 
 def kernel(
     n_row, n_col,
-    vel, dy_hbm, dz_hbm, force, cell,
+    vel, dy_hbm, dz_hbm, force_hbm, cell_hbm,
     out,
-    dy, dz, vw, y_in, z_in, y_out, z_out, y_back, z_back, node_tile, node_all, delta,
+    dy, dz, force, cell, vw, y_in, z_in, y_out, z_out, y_back, z_back, node_tile, node_all, delta,
     load_sem, y_in_sem, z_in_sem, y_back_sem, z_back_sem, node_sem,
     y_in_send, z_in_send, y_back_send, z_back_send, node_send,
 ):
@@ -25,7 +25,7 @@
     c = lax.axis_index("col")
     ny, nz = vel.shape[2], vel.shape[3]
     planes = vel.shape[1] // n_col
-    n_nodes = force.shape[1]
+    n_nodes = force_hbm.shape[1]
 
     barrier = pltpu.get_barrier_semaphore()
 
@@ -44,11 +44,17 @@
     load_dy = pltpu.make_async_copy(dy_hbm, dy, load_sem.at[0])
     load_dz = pltpu.make_async_copy(dz_hbm, dz, load_sem.at[1])
     load_vw = pltpu.make_async_copy(vel.at[pl.ds(1, 2)], vw, load_sem.at[2])
+    load_force = pltpu.make_async_copy(force_hbm, force, load_sem.at[3])
+    load_cell = pltpu.make_async_copy(cell_hbm, cell, load_sem.at[4])
+    load_force.start()
+    load_cell.start()
 
     group = (n_row * n_nodes) // 128
     per_tile = n_row // group
     lane = lax.broadcasted_iota(jnp.int32, (COMPS, 128), 1)
     base = lax.rem(r, per_tile) * n_nodes
+    load_force.wait()
+    load_cell.wait()
     forces, cells = force[...], cell[...].astype(F32)
     spread_f = jnp.zeros((COMPS, 128), F32)
     spread_c = jnp.zeros((COMPS, 128), F32)
@@ -222,16 +228,18 @@
     _, n_x, ny, nz = velocity.shape
     planes = n_x // n_col
     dma = pltpu.SemaphoreType.DMA
-    hbm = pl.BlockSpec(memory_space=pl.ANY)
+    hbm = pl.BlockSpec(memory_space=pltpu.HBM)
     vmem = pl.BlockSpec(memory_space=pltpu.VMEM)
     return pl.pallas_call(
         functools.partial(kernel, n_row, n_col),
         out_shape=jax.ShapeDtypeStruct(velocity.shape, F32),
-        in_specs=[hbm, hbm, hbm, vmem, vmem],
+        in_specs=[hbm] * 5,
         out_specs=vmem,
         scratch_shapes=[
             pltpu.VMEM(dy_op.shape, BF16),
             pltpu.VMEM(dz_op.shape, BF16),
+            pltpu.VMEM(node_force.shape, F32),
+            pltpu.VMEM(node_cell.shape, jnp.int32),
             pltpu.VMEM((2, n_x, ny, nz), F32),
             pltpu.VMEM((COMPS, n_row * ny, nz), F32),
             pltpu.VMEM((COMPS, n_col, planes, ny, nz), F32),
@@ -242,11 +250,11 @@
             pltpu.VMEM((8, 128), F32),
             pltpu.VMEM((n_row, 8, 128), F32),
             pltpu.VMEM((COMPS, n_x * ny, nz), F32),
-            dma((3,)), dma((COMPS,)), dma((COMPS,)), dma((COMPS,)), dma((COMPS,)), dma(()),
+            dma((5,)), dma((COMPS,)), dma((COMPS,)), dma((COMPS,)), dma((COMPS,)), dma(()),
             dma((COMPS,)), dma((COMPS,)), dma((COMPS,)), dma((COMPS,)), dma(()),
         ],
         compiler_params=pltpu.CompilerParams(
-            collective_id=0, has_side_effects=True, vmem_limit_bytes=48 * 1024 * 1024
+            collective_id=0, has_side_effects=True, vmem_limit_bytes=56 * 1024 * 1024
         ),
     )(velocity, dy_op, dz_op, node_force, node_cell)
 

time: 90.6 us -> 89.2 us (0.985)
  local copies, waits for them, and re-layouts: 5.51 us -> 2.67 us
  Pallas kernels: 84.9 us -> 86.4 us
    unnamed x9 -> x1, local copies, waits for them, and re-layouts: 5.51 us -> 2.67 us
    pallas_call x1, Pallas kernels: 84.9 us -> 86.4 us  [per_device(): pl.pallas_call(functools.partial(kernel, n_row, n_col), out_shape=jax.Sha...]
where the time goes in v2:
time: 89.2 us; the launch traced here: 89.1 us
  Pallas kernels  86.4 us (97%)
  local copies, waits for them, and re-layouts  2.67 us (3%)
    pallas_call x1, Pallas kernels, per_device(): pl.pallas_call(functools.partial(kernel, n_row, n_col), out_shape=jax.Sha...  86.4 us
    unnamed x1, local copies, waits for them, and re-layouts  2.67 us

profile of v2, /device:TPU:1, one launch (start us, length us, event | category | flops | bytes accessed | tf_op | source)
XLA Modules:
  0.0 89.1 jit_solution(4933139721948663870)
XLA Ops:
  0.0 86.4 %shard_map.55 = f32[3,32,32,128]{3,2,1,0:T(8,128)} custom-call(f32[3,32,32,128]{3,2,1,0:T(8,128)} %vel.1, bf16[1024,1024]{1,0:T(8,128)(2,1)} %dy_hbm.1, bf16[1024,1024]{1,0:T(8,128)(2,1)} %dz_hbm.1, f32[3,8]{1,0:T(4,128)} %force_hbm.1, s32[3,8]{1,0:T(4,128)} %cell_hbm.1), custom_call_target="tpu_custom_call" | custom-call | tf_op jit(solution)/shard_map/pallas_call | solution.py:233
  86.4 2.7 %copy.7 = f32[3,32,32,128]{3,2,1,0:T(8,128)} copy(f32[3,32,32,128]{3,2,1,0:T(8,128)} %shard_map.55) | data formatting | bytes 3145728

commit v3 on v2

v3 whole, which is shorter than its diff:
```python
import functools

import jax
import jax.numpy as jnp
from jax import lax
from jax.experimental import pallas as pl
from jax.experimental.pallas import tpu as pltpu
from jax.sharding import PartitionSpec as P

MESH = pl.DeviceIdType.MESH
F32 = jnp.float32
BF16 = jnp.bfloat16
COMPS = 3
GROUP = 4


def wait_for(ref, sem):
    pltpu.make_async_copy(ref, ref, sem).wait()


def kernel(
    n_row, n_col,
    vel, dy_hbm, dz_hbm, force_hbm, cell_hbm,
    out,
    dy, dz, force, cell, vw,
    by_z, y_in, y_out, by_group, y_back, z_in, z_out, z_back,
    node_tile, node_z, node_all, delta,
    load_sem, by_z_sem, y_in_sem, by_group_sem, y_back_sem, z_in_sem, z_back_sem, node_sem,
    by_z_send, y_in_send, by_group_send, y_back_send, z_in_send, z_back_send, node_send,
):
    n_z = n_row // GROUP
    r = lax.axis_index("row")
    c = lax.axis_index("col")
    z, q = r // GROUP, r % GROUP
    ny, nz = vel.shape[2], vel.shape[3]
    planes = vel.shape[1] // n_col
    n_nodes = force_hbm.shape[1]
    z_offsets = sorted(range(1, n_z), key=lambda d: -min(d, n_z - d))

    def along_z(d):
        return (z + d) % n_z

    def in_group(d):
        return (q + d) % GROUP

    def along_col(d):
        return (c + d) % n_col

    def send(src, dst, send_sem, recv_sem, **to):
        pltpu.make_async_remote_copy(
            src_ref=src, dst_ref=dst, send_sem=send_sem, recv_sem=recv_sem,
            device_id=to, device_id_type=MESH,
        ).start()

    barrier = pltpu.get_barrier_semaphore()
    for d in z_offsets:
        pl.semaphore_signal(
            barrier, inc=1, device_id={"row": along_z(d) * GROUP + q}, device_id_type=MESH
        )
    for d in range(1, n_col):
        pl.semaphore_signal(barrier, inc=1, device_id={"col": along_col(d)}, device_id_type=MESH)
    for d in range(1, GROUP):
        pl.semaphore_signal(
            barrier, inc=1, device_id={"row": z * GROUP + in_group(d)}, device_id_type=MESH
        )

    load_dy = pltpu.make_async_copy(dy_hbm, dy, load_sem.at[0])
    load_dz = pltpu.make_async_copy(dz_hbm, dz, load_sem.at[1])
    load_vw = pltpu.make_async_copy(vel.at[pl.ds(1, 2)], vw, load_sem.at[2])
    load_force = pltpu.make_async_copy(force_hbm, force, load_sem.at[3])
    load_cell = pltpu.make_async_copy(cell_hbm, cell, load_sem.at[4])
    load_force.start()
    load_cell.start()
    for k in range(COMPS):
        pltpu.make_async_copy(
            vel.at[k, pl.ds(z * GROUP, GROUP)], by_z.at[k, z], by_z_sem.at[k]
        ).start()
        pltpu.make_async_copy(
            vel.at[k, pl.ds(c * planes, planes)], z_in.at[k, c], z_in_sem.at[k]
        ).start()
    load_dz.start()
    load_dy.start()
    load_vw.start()

    pl.semaphore_wait(barrier, n_z + n_col + GROUP - 3)

    def z_forward(k):
        for d in z_offsets:
            to = along_z(d)
            send(
                vel.at[k, pl.ds(to * GROUP, GROUP)], by_z.at[k, z],
                by_z_send.at[k], by_z_sem.at[k], row=to * GROUP + q,
            )

    def group_forward(k):
        wait_for(by_z.at[k], by_z_sem.at[k])
        for d in range(1, GROUP):
            to = in_group(d)
            send(
                by_z.at[k, :, to], y_in.at[k, :, q],
                y_in_send.at[k], y_in_sem.at[k], row=z * GROUP + to,
            )
        pltpu.make_async_copy(by_z.at[k, :, q], y_in.at[k, :, q], y_in_sem.at[k]).start()

    def y_gradient(k):
        wait_for(y_in.at[k], y_in_sem.at[k])
        lines = y_in[k].reshape(n_row * ny, nz).astype(BF16)
        rows = 2 * GROUP * ny
        for m in range(n_z // 2):
            y_out[k, 2 * m : 2 * m + 2] = jnp.dot(
                dy[m * rows : (m + 1) * rows, :], lines, preferred_element_type=F32
            ).reshape(2, GROUP, ny, nz)
        for d in range(1, GROUP):
            to = in_group(d)
            send(
                y_out.at[k, :, to], by_group.at[k, :, q],
                by_group_send.at[k], by_group_sem.at[k], row=z * GROUP + to,
            )
        pltpu.make_async_copy(
            y_out.at[k, :, q], by_group.at[k, :, q], by_group_sem.at[k]
        ).start()

    def z_return(k):
        wait_for(by_group.at[k], by_group_sem.at[k])
        for d in z_offsets:
            to = along_z(d)
            send(
                by_group.at[k, to], y_back.at[k, pl.ds(z * GROUP, GROUP)],
                y_back_send.at[k], y_back_sem.at[k], row=to * GROUP + q,
            )
        pltpu.make_async_copy(
            by_group.at[k, z], y_back.at[k, pl.ds(z * GROUP, GROUP)], y_back_sem.at[k]
        ).start()

    def col_forward(k):
        for d in range(1, n_col):
            to = along_col(d)
            send(
                vel.at[k, pl.ds(to * planes, planes)], z_in.at[k, c],
                z_in_send.at[k], z_in_sem.at[k], col=to,
            )

    def z_gradient(k):
        wait_for(z_in.at[k], z_in_sem.at[k])
        lines = jnp.concatenate(
            [z_in[k, j].reshape(planes * ny, nz) for j in range(n_col)], axis=1
        ).astype(BF16)
        for j in range(n_col):
            z_out[k, j] = lax.dot_general(
                lines, dz[j * nz : (j + 1) * nz, :], (((1,), (1,)), ((), ())),
                preferred_element_type=F32,
            ).reshape(planes, ny, nz)

    def col_return(k):
        for d in range(1, n_col):
            to = along_col(d)
            send(
                z_out.at[k, to], z_back.at[k, pl.ds(c * planes, planes)],
                z_back_send.at[k], z_back_sem.at[k], col=to,
            )
        pltpu.make_async_copy(
            z_out.at[k, c], z_back.at[k, pl.ds(c * planes, planes)], z_back_sem.at[k]
        ).start()

    for k in range(COMPS):
        z_forward(k)
    for k in range(COMPS):
        col_forward(k)

    group = (n_row * n_nodes) // 128
    per_tile = n_row // group
    lane = lax.broadcasted_iota(jnp.int32, (COMPS, 128), 1)
    base = (r % per_tile) * n_nodes
    load_force.wait()
    load_cell.wait()
    forces, cells = force[...], cell[...].astype(F32)
    spread_f = jnp.zeros((COMPS, 128), F32)
    spread_c = jnp.zeros((COMPS, 128), F32)
    for k in range(n_nodes):
        spread_f = jnp.where(lane == base + k, forces[:, k : k + 1], spread_f)
        spread_c = jnp.where(lane == base + k, cells[:, k : k + 1], spread_c)
    node_tile[...] = jnp.zeros_like(node_tile)
    node_tile[0:COMPS, :] = spread_f
    node_tile[4 : 4 + COMPS, :] = spread_c
    for d in z_offsets:
        send(
            node_tile, node_z.at[z], node_send.at[0], node_sem.at[0],
            row=along_z(d) * GROUP + q,
        )
    pltpu.make_async_copy(node_tile, node_z.at[z], node_sem.at[0]).start()

    load_dz.wait()
    load_dy.wait()
    group_forward(0)
    z_gradient(0)
    y_gradient(0)
    z_gradient(1)
    group_forward(1)
    z_return(0)
    z_gradient(2)
    y_gradient(1)
    group_forward(2)
    z_return(1)

    wait_for(node_z, node_sem.at[0])
    for d in range(1, GROUP):
        send(
            node_z, node_all.at[q], node_send.at[1], node_sem.at[1],
            row=z * GROUP + in_group(d),
        )
    pltpu.make_async_copy(node_z, node_all.at[q], node_sem.at[1]).start()

    y_gradient(2)
    for k in range(COMPS):
        col_return(k)
    z_return(2)

    wait_for(node_all, node_sem.at[1])
    tiles = []
    z_per_tile = per_tile // GROUP
    for g in range(group):
        total = node_all[0, g * z_per_tile]
        for j in range(GROUP):
            for i in range(z_per_tile):
                if i or j:
                    total = total + node_all[j, g * z_per_tile + i]
        tiles.append(total)
    nodes = jnp.concatenate(tiles, axis=1)
    count = 128 * group
    first_y = (r * ny).astype(F32)
    first_z = (c * nz).astype(F32)
    local_y = nodes[5:6, :] - first_y
    owned = (local_y >= 0.0) & (local_y < float(ny))
    key = jnp.where(owned, nodes[4:5, :] * float(ny) + local_y, -1.0)
    key_z = nodes[6:7, :] - first_z
    z_pos = lax.broadcasted_iota(jnp.int32, (nz, count), 0).astype(F32)
    hot_z = jnp.where(z_pos == key_z, 1.0, 0.0).astype(BF16)
    high = nodes.astype(BF16).astype(F32)
    rest = nodes - high
    mid = rest.astype(BF16).astype(F32)
    low = rest - mid
    rows = vel.shape[1] * ny
    step = 256 if rows % 256 == 0 else rows

    @pl.loop(0, rows // step)
    def _(m):
        pos = (lax.broadcasted_iota(jnp.int32, (step, count), 0) + m * step).astype(F32)
        hit = pos == key
        for k in range(COMPS):
            total = jnp.zeros((step, nz), F32)
            for part in (high, mid, low):
                pushed = jnp.where(hit, part[k : k + 1, :], 0.0).astype(BF16)
                total = total + lax.dot_general(
                    pushed, hot_z, (((1,), (1,)), ((), ())), preferred_element_type=F32
                )
            delta[k, pl.ds(pl.multiple_of(m * step, step), step), :] = total

    load_vw.wait()
    for k in range(COMPS):
        wait_for(z_back.at[k], z_back_sem.at[k])
        wait_for(y_back.at[k], y_back_sem.at[k])
        out[k] = delta[k].reshape(out.shape[1:]) - (vw[0] * y_back[k] + vw[1] * z_back[k])

    for k in range(COMPS):
        z_sent = by_z.at[k, pl.ds(0, n_z - 1)]
        group_sent = by_z.at[k, :, pl.ds(0, GROUP - 1)]
        col_sent = z_in.at[k, pl.ds(0, n_col - 1)]
        wait_for(z_sent, by_z_send.at[k])
        wait_for(group_sent, y_in_send.at[k])
        wait_for(group_sent, by_group_send.at[k])
        wait_for(z_sent, y_back_send.at[k])
        wait_for(col_sent, z_in_send.at[k])
        wait_for(col_sent, z_back_send.at[k])
    wait_for(node_z.at[pl.ds(0, n_z - 1)], node_send.at[0])
    wait_for(node_all.at[pl.ds(0, GROUP - 1)], node_send.at[1])


def per_device(n_row, n_col, velocity, dy_op, dz_op, node_force, node_cell):
    _, n_x, ny, nz = velocity.shape
    planes = n_x // n_col
    n_z = n_row // GROUP
    dma = pltpu.SemaphoreType.DMA
    hbm = pl.BlockSpec(memory_space=pltpu.HBM)
    vmem = pl.BlockSpec(memory_space=pltpu.VMEM)
    lines = pltpu.VMEM((COMPS, n_z, GROUP, ny, nz), F32)
    owned = pltpu.VMEM((COMPS, n_x, ny, nz), F32)
    col_lines = pltpu.VMEM((COMPS, n_col, planes, ny, nz), F32)
    return pl.pallas_call(
        functools.partial(kernel, n_row, n_col),
        out_shape=jax.ShapeDtypeStruct(velocity.shape, F32),
        in_specs=[hbm] * 5,
        out_specs=vmem,
        scratch_shapes=[
            pltpu.VMEM(dy_op.shape, BF16),
            pltpu.VMEM(dz_op.shape, BF16),
            pltpu.VMEM(node_force.shape, F32),
            pltpu.VMEM(node_cell.shape, jnp.int32),
            pltpu.VMEM((2, n_x, ny, nz), F32),
            lines, lines, lines, lines, owned, col_lines, col_lines, owned,
            pltpu.VMEM((8, 128), F32),
            pltpu.VMEM((n_z, 8, 128), F32),
            pltpu.VMEM((GROUP, n_z, 8, 128), F32),
            pltpu.VMEM((COMPS, n_x * ny, nz), F32),
            dma((5,)), *[dma((COMPS,))] * 6, dma((2,)),
            *[dma((COMPS,))] * 6, dma((2,)),
        ],
        compiler_params=pltpu.CompilerParams(
            collective_id=0, has_side_effects=True, vmem_limit_bytes=40 * 1024 * 1024
        ),
    )(*(
        pltpu.with_memory_space_constraint(x, pltpu.HBM)
        for x in (velocity, dy_op, dz_op, node_force, node_cell)
    ))


def solution(mesh):
    return jax.shard_map(
        functools.partial(per_device, mesh.shape["row"], mesh.shape["col"]),
        mesh=mesh,
        in_specs=(
            P(None, None, "row", "col"),
            P(),
            P(),
            P(None, ("row", "col")),
            P(None, ("row", "col")),
        ),
        out_specs=P(None, None, "row", "col"),
        check_vma=False,
    )
```

time: 89.2 us -> 93.3 us (1.046)
  Pallas kernels: 86.4 us -> 92.1 us
  local copies, waits for them, and re-layouts: 2.67 us -> 1.15 us
    pallas_call x1, Pallas kernels: 86.4 us -> 92.1 us  [per_device(): pl.pallas_call(functools.partial(kernel, n_row, n_col), out_shape=jax.Sha...]
    unnamed x1, local copies, waits for them, and re-layouts: 2.67 us -> 1.15 us
where the time goes in v3:
time: 93.3 us
  Pallas kernels  92.1 us (99%)
  local copies, waits for them, and re-layouts  1.15 us (1%)
    pallas_call x1, Pallas kernels, per_device(): pl.pallas_call(functools.partial(kernel, n_row, n_col), out_shape=jax.Sha...  92.1 us

profile of v3, /device:TPU:1, one launch (start us, length us, event | category | flops | bytes accessed | tf_op | source)
XLA Modules:
  0.0 93.3 jit_solution(9161310223150435476)
XLA Ops:
  0.0 92.1 %shard_map.55 = f32[3,32,32,128]{3,2,1,0:T(8,128)S(1)} custom-call(f32[3,32,32,128]{3,2,1,0:T(8,128)} %vel.1, bf16[1024,1024]{1,0:T(8,128)(2,1)} %dy_hbm.1, bf16[1024,1024]{1,0:T(8,128)(2,1)} %dz_hbm.1, f32[3,8]{1,0:T(4,128)} %force_hbm.1, s32[3,8]{1,0:T(4,128)} %cell_hbm.1), custom_call_target="tpu_custom_call" | custom-call | tf_op jit(solution)/shard_map/pallas_call | solution.py:288
  92.1 1.1 %copy.7 = f32[3,32,32,128]{3,2,1,0:T(8,128)} copy(f32[3,32,32,128]{3,2,1,0:T(8,128)S(1)} %shard_map.55) | data formatting | bytes 3145728

commit v4 on v2

--- a/solution.py
+++ b/solution.py
@@ -11,6 +11,12 @@
 F32 = jnp.float32
 BF16 = jnp.bfloat16
 COMPS = 3
+GROUP = 4
+RETURN_ORDER = (0, 1, 2, 4, 3, 7, 6, 5)
+
+
+def return_order(n_z):
+    return [p for p in RETURN_ORDER if p < n_z] + list(range(len(RETURN_ORDER), n_z))
 
 
 def kernel(
@@ -128,9 +134,7 @@
                 dy[m * rows : (m + 1) * rows, :], lines, preferred_element_type=F32
             )
 
-        @pl.loop(1, n_row)
-        def _(s):
-            to = lax.rem(r + s, n_row)
+        def y_return(to):
             pltpu.make_async_remote_copy(
                 src_ref=y_out.at[k, pl.ds(pl.multiple_of(to * ny, ny), ny)],
                 dst_ref=y_back.at[k, r],
@@ -139,6 +143,16 @@
                 device_id={"row": to},
                 device_id_type=MESH,
             ).start()
+
+        for to_z in return_order(n_row // GROUP):
+
+            @pl.loop(0, GROUP)
+            def _(s):
+                to = to_z * GROUP + lax.rem(r + s, GROUP)
+
+                @pl.when(to != r)
+                def _():
+                    y_return(to)
 
         pltpu.make_async_copy(
             y_out.at[k, pl.ds(pl.multiple_of(r * ny, ny), ny)], y_back.at[k, r], y_back_sem.at[k]
@@ -254,9 +268,12 @@
             dma((COMPS,)), dma((COMPS,)), dma((COMPS,)), dma((COMPS,)), dma(()),
         ],
         compiler_params=pltpu.CompilerParams(
-            collective_id=0, has_side_effects=True, vmem_limit_bytes=56 * 1024 * 1024
+            collective_id=0, has_side_effects=True, vmem_limit_bytes=40 * 1024 * 1024
         ),
-    )(velocity, dy_op, dz_op, node_force, node_cell)
+    )(*(
+        pltpu.with_memory_space_constraint(x, pltpu.HBM)
+        for x in (velocity, dy_op, dz_op, node_force, node_cell)
+    ))
 
 
 def solution(mesh):

time: 89.2 us -> 85.3 us (0.956)
  Pallas kernels: 86.4 us -> 84.1 us
  local copies, waits for them, and re-layouts: 2.67 us -> 1.15 us
    pallas_call x1, Pallas kernels: 86.4 us -> 84.1 us  [per_device(): pl.pallas_call(functools.partial(kernel, n_row, n_col), out_shape=jax.Sha...]
    unnamed x1, local copies, waits for them, and re-layouts: 2.67 us -> 1.15 us
where the time goes in v4:
time: 85.3 us; the launch traced here: 85.2 us
  Pallas kernels  84.1 us (99%)
  local copies, waits for them, and re-layouts  1.15 us (1%)
    pallas_call x1, Pallas kernels, per_device(): pl.pallas_call(functools.partial(kernel, n_row, n_col), out_shape=jax.Sha...  84.1 us

profile of v4, /device:TPU:1, one launch (start us, length us, event | category | flops | bytes accessed | tf_op | source)
XLA Modules:
  0.0 85.2 jit_solution(17236628543148438019)
XLA Ops:
  0.0 84.1 %shard_map.55 = f32[3,32,32,128]{3,2,1,0:T(8,128)S(1)} custom-call(f32[3,32,32,128]{3,2,1,0:T(8,128)} %vel.1, bf16[1024,1024]{1,0:T(8,128)(2,1)} %dy_hbm.1, bf16[1024,1024]{1,0:T(8,128)(2,1)} %dz_hbm.1, f32[3,8]{1,0:T(4,128)} %force_hbm.1, s32[3,8]{1,0:T(4,128)} %cell_hbm.1), custom_call_target="tpu_custom_call" | custom-call | tf_op jit(solution)/shard_map/pallas_call | solution.py:247
  84.1 1.1 %copy.7 = f32[3,32,32,128]{3,2,1,0:T(8,128)} copy(f32[3,32,32,128]{3,2,1,0:T(8,128)S(1)} %shard_map.55) | data formatting | bytes 3145728

commit v5 on v4

--- a/solution.py
+++ b/solution.py
@@ -23,7 +23,7 @@
     n_row, n_col,
     vel, dy_hbm, dz_hbm, force_hbm, cell_hbm,
     out,
-    dy, dz, force, cell, vw, y_in, z_in, y_out, z_out, y_back, z_back, node_tile, node_all, delta,
+    dy, dz, force, cell, vw, y_in, z_in, y_out, z_out, y_back, z_back, node_tile, node_z, node_sum, node_all, delta,
     load_sem, y_in_sem, z_in_sem, y_back_sem, z_back_sem, node_sem,
     y_in_send, z_in_send, y_back_send, z_back_send, node_send,
 ):
@@ -35,16 +35,15 @@
 
     barrier = pltpu.get_barrier_semaphore()
 
-    @pl.loop(1, n_row)
-    def _(s):
+    n_z = n_row // GROUP
+    for d in sorted(range(n_z), key=lambda d: -min(d, n_z - d)):
+        for e in range(GROUP):
+            if d or e:
+                to = lax.rem(r // GROUP + d, n_z) * GROUP + lax.rem(r + e, GROUP)
+                pl.semaphore_signal(barrier, inc=1, device_id={"row": to}, device_id_type=MESH)
+    for d in range(1, n_col):
         pl.semaphore_signal(
-            barrier, inc=1, device_id={"row": lax.rem(r + s, n_row)}, device_id_type=MESH
-        )
-
-    @pl.loop(1, n_col)
-    def _(s):
-        pl.semaphore_signal(
-            barrier, inc=1, device_id={"col": lax.rem(c + s, n_col)}, device_id_type=MESH
+            barrier, inc=1, device_id={"col": lax.rem(c + d, n_col)}, device_id_type=MESH
         )
 
     load_dy = pltpu.make_async_copy(dy_hbm, dy, load_sem.at[0])
@@ -110,22 +109,22 @@
             load_dz.start()
             load_vw.start()
 
-            @pl.loop(1, n_row)
-            def _(s):
+            for d in range(1, n_z):
+                to_z = lax.rem(r // GROUP + d, n_z)
                 pltpu.make_async_remote_copy(
                     src_ref=node_tile,
-                    dst_ref=node_all.at[r],
-                    send_sem=node_send,
-                    recv_sem=node_sem,
-                    device_id={"row": lax.rem(r + s, n_row)},
+                    dst_ref=node_z.at[r // GROUP],
+                    send_sem=node_send.at[0],
+                    recv_sem=node_sem.at[0],
+                    device_id={"row": to_z * GROUP + lax.rem(r, GROUP)},
                     device_id_type=MESH,
                 ).start()
 
-            pltpu.make_async_copy(node_tile, node_all.at[r], node_sem).start()
+            pltpu.make_async_copy(node_tile, node_z.at[r // GROUP], node_sem.at[0]).start()
 
     load_dy.wait()
     load_dz.wait()
-    for k in range(COMPS):
+    def y_part(k):
         pltpu.make_async_copy(y_in.at[k], y_in.at[k], y_in_sem.at[k]).wait()
         lines = y_in[k].astype(BF16)
         rows = 256 if dy.shape[0] % 256 == 0 else dy.shape[0]
@@ -158,6 +157,7 @@
             y_out.at[k, pl.ds(pl.multiple_of(r * ny, ny), ny)], y_back.at[k, r], y_back_sem.at[k]
         ).start()
 
+    def z_part(k):
         pltpu.make_async_copy(z_in.at[k], z_in.at[k], z_in_sem.at[k]).wait()
         lines = jnp.concatenate(
             [z_in[k, j].reshape(planes * ny, nz) for j in range(n_col)], axis=1
@@ -184,12 +184,37 @@
             z_out.at[k, c], z_back.at[k, pl.ds(c * planes, planes)], z_back_sem.at[k]
         ).start()
 
-    pltpu.make_async_copy(node_all, node_all, node_sem).wait()
+    y_part(0)
+    z_part(0)
+    pltpu.make_async_copy(node_z, node_z, node_sem.at[0]).wait()
+    z_per_tile = per_tile // GROUP
+    for g in range(group):
+        total = node_z[g * z_per_tile]
+        for j in range(1, z_per_tile):
+            total = total + node_z[g * z_per_tile + j]
+        node_sum[g] = total
+    for d in range(1, GROUP):
+        to_q = lax.rem(r + d, GROUP)
+        pltpu.make_async_remote_copy(
+            src_ref=node_sum,
+            dst_ref=node_all.at[lax.rem(r, GROUP)],
+            send_sem=node_send.at[1],
+            recv_sem=node_sem.at[1],
+            device_id={"row": r // GROUP * GROUP + to_q},
+            device_id_type=MESH,
+        ).start()
+    pltpu.make_async_copy(node_sum, node_all.at[lax.rem(r, GROUP)], node_sem.at[1]).start()
+    y_part(1)
+    y_part(2)
+    z_part(1)
+    z_part(2)
+
+    pltpu.make_async_copy(node_all, node_all, node_sem.at[1]).wait()
     tiles = []
     for g in range(group):
-        total = node_all[g * per_tile]
-        for j in range(1, per_tile):
-            total = total + node_all[g * per_tile + j]
+        total = node_all[0, g]
+        for j in range(1, GROUP):
+            total = total + node_all[j, g]
         tiles.append(total)
     nodes = jnp.concatenate(tiles, axis=1)
     count = 128 * group
@@ -234,13 +259,16 @@
         pltpu.make_async_copy(z_sent, z_sent, z_in_send.at[k]).wait()
         pltpu.make_async_copy(y_sent, y_sent, y_back_send.at[k]).wait()
         pltpu.make_async_copy(z_sent, z_sent, z_back_send.at[k]).wait()
-    nodes_sent = node_all.at[pl.ds(0, n_row - 1)]
-    pltpu.make_async_copy(nodes_sent, nodes_sent, node_send).wait()
+    z_sent = node_z.at[pl.ds(0, n_z - 1)]
+    group_sent = node_all.at[pl.ds(0, GROUP - 1)]
+    pltpu.make_async_copy(z_sent, z_sent, node_send.at[0]).wait()
+    pltpu.make_async_copy(group_sent, group_sent, node_send.at[1]).wait()
 
 
 def per_device(n_row, n_col, velocity, dy_op, dz_op, node_force, node_cell):
     _, n_x, ny, nz = velocity.shape
     planes = n_x // n_col
+    node_tiles = n_row * node_force.shape[1] // 128
     dma = pltpu.SemaphoreType.DMA
     hbm = pl.BlockSpec(memory_space=pltpu.HBM)
     vmem = pl.BlockSpec(memory_space=pltpu.VMEM)
@@ -262,10 +290,12 @@
             pltpu.VMEM((COMPS, n_x, ny, nz), F32),
             pltpu.VMEM((COMPS, n_x, ny, nz), F32),
             pltpu.VMEM((8, 128), F32),
-            pltpu.VMEM((n_row, 8, 128), F32),
+            pltpu.VMEM((n_row // GROUP, 8, 128), F32),
+            pltpu.VMEM((node_tiles, 8, 128), F32),
+            pltpu.VMEM((GROUP, node_tiles, 8, 128), F32),
             pltpu.VMEM((COMPS, n_x * ny, nz), F32),
-            dma((5,)), dma((COMPS,)), dma((COMPS,)), dma((COMPS,)), dma((COMPS,)), dma(()),
-            dma((COMPS,)), dma((COMPS,)), dma((COMPS,)), dma((COMPS,)), dma(()),
+            dma((5,)), dma((COMPS,)), dma((COMPS,)), dma((COMPS,)), dma((COMPS,)), dma((2,)),
+            dma((COMPS,)), dma((COMPS,)), dma((COMPS,)), dma((COMPS,)), dma((2,)),
         ],
         compiler_params=pltpu.CompilerParams(
             collective_id=0, has_side_effects=True, vmem_limit_bytes=40 * 1024 * 1024

time: 85.3 us -> 82.5 us (0.967)
  Pallas kernels: 84.1 us -> 81.2 us
    pallas_call x1, Pallas kernels: 84.1 us -> 81.2 us  [per_device(): pl.pallas_call(functools.partial(kernel, n_row, n_col), out_shape=jax.Sha...]
where the time goes in v5:
time: 82.5 us; the launch traced here: 82.4 us
  Pallas kernels  81.2 us (98%)
  local copies, waits for them, and re-layouts  1.15 us (1%)
    pallas_call x1, Pallas kernels, per_device(): pl.pallas_call(functools.partial(kernel, n_row, n_col), out_shape=jax.Sha...  81.2 us

profile of v5, /device:TPU:1, one launch (start us, length us, event | category | flops | bytes accessed | tf_op | source)
XLA Modules:
  0.0 82.4 jit_solution(18081938730180269689)
XLA Ops:
  0.0 81.2 %shard_map.55 = f32[3,32,32,128]{3,2,1,0:T(8,128)S(1)} custom-call(f32[3,32,32,128]{3,2,1,0:T(8,128)} %vel.1, bf16[1024,1024]{1,0:T(8,128)(2,1)} %dy_hbm.1, bf16[1024,1024]{1,0:T(8,128)(2,1)} %dz_hbm.1, f32[3,8]{1,0:T(4,128)} %force_hbm.1, s32[3,8]{1,0:T(4,128)} %cell_hbm.1), custom_call_target="tpu_custom_call" | custom-call | tf_op jit(solution)/shard_map/pallas_call | solution.py:275
  81.3 1.1 %copy.7 = f32[3,32,32,128]{3,2,1,0:T(8,128)} copy(f32[3,32,32,128]{3,2,1,0:T(8,128)S(1)} %shard_map.55) | data formatting | bytes 3145728

commit v6 on v5

--- a/solution.py
+++ b/solution.py
@@ -11,8 +11,9 @@
 F32 = jnp.float32
 BF16 = jnp.bfloat16
 COMPS = 3
+PARTS = ((0, 1), (1, 2))
 GROUP = 4
-RETURN_ORDER = (0, 1, 2, 4, 3, 7, 6, 5)
+RETURN_ORDER = (0, 1, 2, 3, 4, 7, 6, 5)
 
 
 def return_order(n_z):
@@ -68,23 +69,28 @@
         spread_c = jnp.where(lane == base + k, cells[:, k : k + 1], spread_c)
     node_tile[...] = jnp.zeros_like(node_tile)
     node_tile[0:COMPS, :] = spread_f
-    node_tile[4 : 4 + COMPS, :] = spread_c
+    node_tile[COMPS : 2 * COMPS, :] = spread_c
 
     pl.semaphore_wait(barrier, n_row + n_col - 2)
 
     for k in range(COMPS):
-
-        @pl.loop(1, n_row)
-        def _(s):
-            to = lax.rem(r + s, n_row)
-            pltpu.make_async_remote_copy(
-                src_ref=vel.at[k, to],
-                dst_ref=y_in.at[k, pl.ds(pl.multiple_of(r * ny, ny), ny)],
-                send_sem=y_in_send.at[k],
-                recv_sem=y_in_sem.at[k],
-                device_id={"row": to},
-                device_id_type=MESH,
-            ).start()
+        if k < len(PARTS):
+            part = pl.ds(*PARTS[k])
+            own = y_in.at[part, pl.ds(pl.multiple_of(r * ny, ny), ny)]
+
+            @pl.loop(1, n_row)
+            def _(s):
+                to = lax.rem(r + s, n_row)
+                pltpu.make_async_remote_copy(
+                    src_ref=vel.at[part, to],
+                    dst_ref=own,
+                    send_sem=y_in_send.at[k],
+                    recv_sem=y_in_sem.at[k],
+                    device_id={"row": to},
+                    device_id_type=MESH,
+                ).start()
+
+            pltpu.make_async_copy(vel.at[part, r], own, y_in_sem.at[k]).start()
 
         @pl.loop(1, n_col)
         def _(s):
@@ -99,9 +105,6 @@
             ).start()
 
         pltpu.make_async_copy(
-            vel.at[k, r], y_in.at[k, pl.ds(pl.multiple_of(r * ny, ny), ny)], y_in_sem.at[k]
-        ).start()
-        pltpu.make_async_copy(
             vel.at[k, pl.ds(c * planes, planes)], z_in.at[k, c], z_in_sem.at[k]
         ).start()
         if k == 0:
@@ -125,18 +128,21 @@
     load_dy.wait()
     load_dz.wait()
     def y_part(k):
-        pltpu.make_async_copy(y_in.at[k], y_in.at[k], y_in_sem.at[k]).wait()
-        lines = y_in[k].astype(BF16)
+        first, n = PARTS[k]
+        part = pl.ds(first, n)
+        pltpu.make_async_copy(y_in.at[part], y_in.at[part], y_in_sem.at[k]).wait()
+        lines = jnp.concatenate([y_in[first + i] for i in range(n)], axis=1).astype(BF16)
         rows = 256 if dy.shape[0] % 256 == 0 else dy.shape[0]
         for m in range(dy.shape[0] // rows):
-            y_out[k, m * rows : (m + 1) * rows, :] = jnp.dot(
-                dy[m * rows : (m + 1) * rows, :], lines, preferred_element_type=F32
-            )
+            span = slice(m * rows, (m + 1) * rows)
+            both = jnp.dot(dy[span, :], lines, preferred_element_type=F32)
+            for i in range(n):
+                y_out[first + i, span, :] = both[:, i * nz : (i + 1) * nz]
 
         def y_return(to):
             pltpu.make_async_remote_copy(
-                src_ref=y_out.at[k, pl.ds(pl.multiple_of(to * ny, ny), ny)],
-                dst_ref=y_back.at[k, r],
+                src_ref=y_out.at[part, pl.ds(pl.multiple_of(to * ny, ny), ny)],
+                dst_ref=y_back.at[part, r],
                 send_sem=y_back_send.at[k],
                 recv_sem=y_back_sem.at[k],
                 device_id={"row": to},
@@ -154,7 +160,8 @@
                     y_return(to)
 
         pltpu.make_async_copy(
-            y_out.at[k, pl.ds(pl.multiple_of(r * ny, ny), ny)], y_back.at[k, r], y_back_sem.at[k]
+            y_out.at[part, pl.ds(pl.multiple_of(r * ny, ny), ny)], y_back.at[part, r],
+            y_back_sem.at[k],
         ).start()
 
     def z_part(k):
@@ -205,7 +212,6 @@
         ).start()
     pltpu.make_async_copy(node_sum, node_all.at[lax.rem(r, GROUP)], node_sem.at[1]).start()
     y_part(1)
-    y_part(2)
     z_part(1)
     z_part(2)
 
@@ -220,10 +226,10 @@
     count = 128 * group
     first_y = (r * ny).astype(F32)
     first_z = (c * nz).astype(F32)
-    local_y = nodes[5:6, :] - first_y
+    local_y = nodes[4:5, :] - first_y
     owned = (local_y >= 0.0) & (local_y < float(ny))
-    key = jnp.where(owned, nodes[4:5, :] * float(ny) + local_y, -1.0)
-    key_z = nodes[6:7, :] - first_z
+    key = jnp.where(owned, nodes[3:4, :] * float(ny) + local_y, -1.0)
+    key_z = nodes[5:6, :] - first_z
     z_pos = lax.broadcasted_iota(jnp.int32, (nz, count), 0).astype(F32)
     hot_z = jnp.where(z_pos == key_z, 1.0, 0.0).astype(BF16)
     high = nodes.astype(BF16).astype(F32)
@@ -248,17 +254,21 @@
 
     load_vw.wait()
     for k in range(COMPS):
-        pltpu.make_async_copy(y_back.at[k], y_back.at[k], y_back_sem.at[k]).wait()
+        if k < len(PARTS):
+            part = pl.ds(*PARTS[k])
+            pltpu.make_async_copy(y_back.at[part], y_back.at[part], y_back_sem.at[k]).wait()
+        out[k] = delta[k].reshape(out.shape[1:]) - vw[0] * y_back[k]
         pltpu.make_async_copy(z_back.at[k], z_back.at[k], z_back_sem.at[k]).wait()
-        out[k] = delta[k].reshape(out.shape[1:]) - (vw[0] * y_back[k] + vw[1] * z_back[k])
+        out[k] = out[k] - vw[1] * z_back[k]
 
     for k in range(COMPS):
-        y_sent = y_in.at[k, pl.ds(0, (n_row - 1) * ny)]
         z_sent = z_in.at[k, pl.ds(0, n_col - 1)]
+        pltpu.make_async_copy(z_sent, z_sent, z_in_send.at[k]).wait()
+        pltpu.make_async_copy(z_sent, z_sent, z_back_send.at[k]).wait()
+    for k in range(len(PARTS)):
+        y_sent = y_in.at[pl.ds(*PARTS[k]), pl.ds(0, (n_row - 1) * ny)]
         pltpu.make_async_copy(y_sent, y_sent, y_in_send.at[k]).wait()
-        pltpu.make_async_copy(z_sent, z_sent, z_in_send.at[k]).wait()
         pltpu.make_async_copy(y_sent, y_sent, y_back_send.at[k]).wait()
-        pltpu.make_async_copy(z_sent, z_sent, z_back_send.at[k]).wait()
     z_sent = node_z.at[pl.ds(0, n_z - 1)]
     group_sent = node_all.at[pl.ds(0, GROUP - 1)]
     pltpu.make_async_copy(z_sent, z_sent, node_send.at[0]).wait()

time: 82.5 us -> 87.6 us (1.062)
  Pallas kernels: 81.2 us -> 86.3 us
    pallas_call x1, Pallas kernels: 81.2 us -> 86.3 us  [per_device(): pl.pallas_call(functools.partial(kernel, n_row, n_col), out_shape=jax.Sha...]
where the time goes in v6:
time: 87.6 us; the launch traced here: 87.5 us
  Pallas kernels  86.3 us (99%)
  local copies, waits for them, and re-layouts  1.15 us (1%)
    pallas_call x1, Pallas kernels, per_device(): pl.pallas_call(functools.partial(kernel, n_row, n_col), out_shape=jax.Sha...  86.3 us

profile of v6, /device:TPU:1, one launch (start us, length us, event | category | flops | bytes accessed | tf_op | source)
XLA Modules:
  0.0 87.5 jit_solution(16737621541691683042)
XLA Ops:
  0.0 86.3 %shard_map.55 = f32[3,32,32,128]{3,2,1,0:T(8,128)S(1)} custom-call(f32[3,32,32,128]{3,2,1,0:T(8,128)} %vel.1, bf16[1024,1024]{1,0:T(8,128)(2,1)} %dy_hbm.1, bf16[1024,1024]{1,0:T(8,128)(2,1)} %dz_hbm.1, f32[3,8]{1,0:T(4,128)} %force_hbm.1, s32[3,8]{1,0:T(4,128)} %cell_hbm.1), custom_call_target="tpu_custom_call" | custom-call | tf_op jit(solution)/shard_map/pallas_call | solution.py:285
  86.3 1.1 %copy.7 = f32[3,32,32,128]{3,2,1,0:T(8,128)} copy(f32[3,32,32,128]{3,2,1,0:T(8,128)S(1)} %shard_map.55) | data formatting | bytes 3145728

commit v7 on v5

--- a/solution.py
+++ b/solution.py
@@ -12,7 +12,7 @@
 BF16 = jnp.bfloat16
 COMPS = 3
 GROUP = 4
-RETURN_ORDER = (0, 1, 2, 4, 3, 7, 6, 5)
+RETURN_ORDER = (0, 1, 2, 3, 4, 7, 6, 5)
 
 
 def return_order(n_z):
@@ -68,12 +68,11 @@
         spread_c = jnp.where(lane == base + k, cells[:, k : k + 1], spread_c)
     node_tile[...] = jnp.zeros_like(node_tile)
     node_tile[0:COMPS, :] = spread_f
-    node_tile[4 : 4 + COMPS, :] = spread_c
+    node_tile[COMPS : 2 * COMPS, :] = spread_c
 
     pl.semaphore_wait(barrier, n_row + n_col - 2)
 
-    for k in range(COMPS):
-
+    def row_forward(k):
         @pl.loop(1, n_row)
         def _(s):
             to = lax.rem(r + s, n_row)
@@ -86,6 +85,7 @@
                 device_id_type=MESH,
             ).start()
 
+    def col_forward(k):
         @pl.loop(1, n_col)
         def _(s):
             to = lax.rem(c + s, n_col)
@@ -98,29 +98,37 @@
                 device_id_type=MESH,
             ).start()
 
+    row_forward(0)
+    col_forward(0)
+    load_dy.start()
+    load_dz.start()
+    load_vw.start()
+
+    for d in range(1, n_z):
+        to_z = lax.rem(r // GROUP + d, n_z)
+        pltpu.make_async_remote_copy(
+            src_ref=node_tile,
+            dst_ref=node_z.at[r // GROUP],
+            send_sem=node_send.at[0],
+            recv_sem=node_sem.at[0],
+            device_id={"row": to_z * GROUP + lax.rem(r, GROUP)},
+            device_id_type=MESH,
+        ).start()
+
+    pltpu.make_async_copy(node_tile, node_z.at[r // GROUP], node_sem.at[0]).start()
+
+    row_forward(1)
+    row_forward(2)
+    col_forward(1)
+    col_forward(2)
+
+    for k in range(COMPS):
         pltpu.make_async_copy(
             vel.at[k, r], y_in.at[k, pl.ds(pl.multiple_of(r * ny, ny), ny)], y_in_sem.at[k]
         ).start()
         pltpu.make_async_copy(
             vel.at[k, pl.ds(c * planes, planes)], z_in.at[k, c], z_in_sem.at[k]
         ).start()
-        if k == 0:
-            load_dy.start()
-            load_dz.start()
-            load_vw.start()
-
-            for d in range(1, n_z):
-                to_z = lax.rem(r // GROUP + d, n_z)
-                pltpu.make_async_remote_copy(
-                    src_ref=node_tile,
-                    dst_ref=node_z.at[r // GROUP],
-                    send_sem=node_send.at[0],
-                    recv_sem=node_sem.at[0],
-                    device_id={"row": to_z * GROUP + lax.rem(r, GROUP)},
-                    device_id_type=MESH,
-                ).start()
-
-            pltpu.make_async_copy(node_tile, node_z.at[r // GROUP], node_sem.at[0]).start()
 
     load_dy.wait()
     load_dz.wait()
@@ -220,10 +228,10 @@
     count = 128 * group
     first_y = (r * ny).astype(F32)
     first_z = (c * nz).astype(F32)
-    local_y = nodes[5:6, :] - first_y
+    local_y = nodes[4:5, :] - first_y
     owned = (local_y >= 0.0) & (local_y < float(ny))
-    key = jnp.where(owned, nodes[4:5, :] * float(ny) + local_y, -1.0)
-    key_z = nodes[6:7, :] - first_z
+    key = jnp.where(owned, nodes[3:4, :] * float(ny) + local_y, -1.0)
+    key_z = nodes[5:6, :] - first_z
     z_pos = lax.broadcasted_iota(jnp.int32, (nz, count), 0).astype(F32)
     hot_z = jnp.where(z_pos == key_z, 1.0, 0.0).astype(BF16)
     high = nodes.astype(BF16).astype(F32)
@@ -249,8 +257,9 @@
     load_vw.wait()
     for k in range(COMPS):
         pltpu.make_async_copy(y_back.at[k], y_back.at[k], y_back_sem.at[k]).wait()
+        out[k] = delta[k].reshape(out.shape[1:]) - vw[0] * y_back[k]
         pltpu.make_async_copy(z_back.at[k], z_back.at[k], z_back_sem.at[k]).wait()
-        out[k] = delta[k].reshape(out.shape[1:]) - (vw[0] * y_back[k] + vw[1] * z_back[k])
+        out[k] = out[k] - vw[1] * z_back[k]
 
     for k in range(COMPS):
         y_sent = y_in.at[k, pl.ds(0, (n_row - 1) * ny)]

time: 82.5 us -> 82.4 us (level)
  no operation moved by 1% of the time
where the time goes in v7:
time: 82.4 us; the launch traced here: 82.1 us
  Pallas kernels  80.9 us (98%)
  local copies, waits for them, and re-layouts  1.15 us (1%)
    pallas_call x1, Pallas kernels, per_device(): pl.pallas_call(functools.partial(kernel, n_row, n_col), out_shape=jax.Sha...  80.9 us

profile of v7, /device:TPU:1, one launch (start us, length us, event | category | flops | bytes accessed | tf_op | source)
XLA Modules:
  0.0 82.1 jit_solution(11690991042941088022)
XLA Ops:
  0.0 80.9 %shard_map.55 = f32[3,32,32,128]{3,2,1,0:T(8,128)S(1)} custom-call(f32[3,32,32,128]{3,2,1,0:T(8,128)} %vel.1, bf16[1024,1024]{1,0:T(8,128)(2,1)} %dy_hbm.1, bf16[1024,1024]{1,0:T(8,128)(2,1)} %dz_hbm.1, f32[3,8]{1,0:T(4,128)} %force_hbm.1, s32[3,8]{1,0:T(4,128)} %cell_hbm.1), custom_call_target="tpu_custom_call" | custom-call | tf_op jit(solution)/shard_map/pallas_call | solution.py:284
  80.9 1.1 %copy.7 = f32[3,32,32,128]{3,2,1,0:T(8,128)} copy(f32[3,32,32,128]{3,2,1,0:T(8,128)S(1)} %shard_map.55) | data formatting | bytes 3145728
